TPU v7x, 32 devices: a whole 2x2x4 slice. The times are simulated.
32 devices in a mesh: level: 2 (over y), sub: 16 (over z, x, core).
Axes of the slice: x: 2, y: 2, z: 4, core: 2. Of those that a mesh axis runs over, the one named last changes fastest.
Arguments:
- factor_inv: float32 [2, 16, 256, 256], P('level', 'sub'), may hold values from -0.0625 to 1.4, as said below
- update_blocks: float32 [2, 16, 4, 128, 256], P('level', 'sub'), may hold values from -0.1875 to 0.1875
- update_rows: int32 [2, 16, 4], P('level', 'sub'), may hold values from 0 to 3, each once within a row
- right_side: float32 [2, 16, 256, 512], P('level', 'sub'), may hold values from -4000 to 4000
Outputs:
- solution: float32 [2, 16, 256, 512], P('level', 'sub')
Inputs may be any that keep to these rules, and one draw needn't show every extreme that they name: `update_rows`: each supernode's 4 update blocks name the 4 target row blocks once each; values below 2 are row blocks of the parent supernode in the same subtree, the others those of the parent supernode in the next subtree (the last subtree's next is the first). `factor_inv`: each 256 x 256 block is lower triangular, with diagonal entries between 0.7 and 1.4.
All inputs are finite; a program needn't handle non-finite values.
Results may differ from a plain program's by a relative error of at most 0.00014.
Values sent between devices are 32-bit elements; how exact they have to be, the bound alone decides.
A program may use at most 64 MiB of HBM per device.

v0:
```python
import jax
import jax.numpy as jnp
from jax import lax
from jax.sharding import PartitionSpec as P

FULL_PRECISION = lax.Precision.HIGHEST


def passed_along(value, axis, steps):
    count = lax.axis_size(axis)
    pairs = [(source, (source + steps) % count) for source in range(count)]
    return lax.ppermute(value, axis, pairs)


def shifted(block, axis, distance):
    devices = range(lax.axis_size(axis))
    route = [(i - distance, i) for i in devices if i - distance in devices]
    return lax.ppermute(block, axis, route)


def apply_plain(matrix, values):
    return jnp.dot(matrix, values, precision=FULL_PRECISION, preferred_element_type=jnp.float32)


def apply_turned(matrix, values):
    return lax.dot_general(
        matrix,
        values,
        (((0,), (0,)), ((), ())),
        precision=FULL_PRECISION,
        preferred_element_type=jnp.float32,
    )


def per_device(factor_inv, update_blocks, update_rows, right_side):
    inverse = factor_inv[0, 0]
    sn_width = inverse.shape[0]
    blocks = update_blocks[0, 0]
    slot_count = blocks.shape[0]
    levels = lax.axis_size("level")
    my_level = lax.axis_index("level")
    slot_table = (
        update_rows[0, 0][:, None] == jnp.arange(slot_count, dtype=jnp.int32)[None, :]
    ).astype(jnp.float32)
    ordered = jnp.einsum("kd,kbj->dbj", slot_table, blocks, precision=FULL_PRECISION).reshape(
        slot_count * blocks.shape[1], sn_width
    )
    own_rows = ordered[:sn_width]
    next_rows = ordered[sn_width:]
    given_rhs = right_side[0, 0]
    partial_value = jnp.sum(given_rhs * given_rhs, axis=0)
    norm_total = lax.psum(partial_value, ("level", "sub"))
    col_scale = jnp.sqrt(norm_total / (levels * lax.axis_size("sub") * sn_width) + 1e-06)
    given_rhs = given_rhs / col_scale
    arrived = jnp.zeros_like(given_rhs)
    forward_all = jnp.zeros_like(given_rhs)
    for step_index in range(levels):
        forward_val = apply_plain(inverse, given_rhs - arrived)
        forward_all = jnp.where(my_level == step_index, forward_val, forward_all)
        if step_index + 1 < levels:
            spread = apply_plain(ordered, forward_val)
            from_left = passed_along(spread[sn_width:], "sub", 1)
            arrived = shifted(spread[:sn_width] + from_left, "level", 1)
    parent_x = jnp.zeros_like(given_rhs)
    result = jnp.zeros_like(given_rhs)
    for step_index in range(levels):
        rhs_block = forward_all
        if step_index > 0:
            beside = passed_along(parent_x, "sub", -1)
            rhs_block = rhs_block - (
                apply_turned(own_rows, parent_x) + apply_turned(next_rows, beside)
            )
        solved = apply_turned(inverse, rhs_block)
        result = jnp.where(my_level == levels - 1 - step_index, solved, result)
        if step_index + 1 < levels:
            parent_x = shifted(solved, "level", -1)
    return result[None, None]


def solution(mesh):
    return jax.shard_map(
        per_device,
        mesh=mesh,
        in_specs=(
            P("level", "sub", None, None),
            P("level", "sub", None, None, None),
            P("level", "sub", None),
            P("level", "sub", None, None),
        ),
        out_specs=P("level", "sub", None, None),
        check_vma=False,
    )
```

profile of v0, /device:TPU:1, one launch (start us, length us, event | category | flops | bytes accessed | tf_op | source)
XLA Modules:
  0.0 98.2 jit_solution(13960839743965393671)
XLA Ops:
  0.0 1.2 %fusion.5 = f32[512]{0:T(512)S(1)} fusion(f32[1,1,256,512]{3,2,1,0:T(8,128)} %param.7), kind=kLoop, calls=%fused_computation.12 | loop fusion | flops 261632 | bytes 526336 | tf_op jit(solution)/shard_map/reduce_sum | solution.py:51
  1.2 40.6 %psum.7 = f32[512]{0:T(512)S(1)} all-reduce(f32[512]{0:T(512)S(1)} %fusion.5), channel_id=1, replica_groups=mesh['level'=2,'sub'=16] {'level','sub'}, use_global_device_ids=true, to_apply=%region_1.0 | all-reduce | flops 512 | bytes 4096 | tf_op jit(solution)/shard_map/psum | solution.py:52
  41.8 0.7 copy-done.3
  42.4 0.9 fusion.8
  43.3 0.1 copy.8
  43.5 0.8 copy-done.1
  44.3 0.2 copy-done.2
  44.4 1.0 %fusion.3 = f32[512,256]{1,0:T(8,128)S(1)} fusion(f32[1,1,256,512]{3,2,1,0:T(8,128)S(1)} %copy-done.2, f32[1,1,256,256]{3,2,1,0:T(8,128)S(1)} %copy-done.1, f32[512]{0:T(512)S(1)} %add_sqrt_fusion), kind=kOutput, calls=%fused_computation.8 | convolution fusion | flops 402784256 | bytes 1312768 | tf_op jit(solution)/shard_map/dot_general | solution.py:22
  45.5 1.0 %fusion.21 = f32[512,512]{1,0:T(8,128)S(1)} fusion(f32[512,256]{1,0:T(8,128)S(1)} %bitcast.49, f32[512,256]{1,0:T(8,128)S(1)} %fusion.3), kind=kOutput, calls=%fused_computation.28 | convolution fusion | flops 805306368 | bytes 2097152 | tf_op jit(solution)/shard_map/dot_general | solution.py:22
  46.5 3.4 %collective-permute-start = (f32[256,512]{1,0:T(8,128)S(1)}, f32[256,512]{1,0:T(8,128)S(1)}, u32[]{:S(2)}, u32[]{:S(2)}) collective-permute-start(f32[256,512]{1,0:T(8,128)S(1)} %slice.25), channel_id=1, source_target_pairs={{0,1},{1,2},{2,3},{3,4},{4,5},{5,6},{6,7},{7,8},{8,9},{9,10},{10,1... | collective-permute-start | bytes 1572872 | tf_op jit(solution)/shard_map/ppermute | solution.py:12
  50.0 6.1 %collective-permute-done = f32[256,512]{1,0:T(8,128)S(1)} collective-permute-done((f32[256,512]{1,0:T(8,128)S(1)}, f32[256,512]{1,0:T(8,128)S(1)}, u32[]{:S(2)}, u32[]{:S(2)}) %collective-permute-start) | collective-permute-done | bytes 524320 | tf_op jit(solution)/shard_map/ppermute | solution.py:12
  56.2 2.2 %collective-permute-start.1 = (f32[256,512]{1,0:T(8,128)S(1)}, f32[256,512]{1,0:T(8,128)S(1)}, u32[]{:S(2)}, u32[]{:S(2)}) collective-permute-start(f32[256,512]{1,0:T(8,128)S(1)} %slice_add_fusion), channel_id=1, source_target_pairs={{0,16},{1,17},{2,18},{3,19},{4,20},{5,21},{6,22},{7,23},{8,24},{9,... | collective-permute-start | bytes 1572872 | tf_op jit(solution)/shard_map/ppermute | solution.py:18
  58.4 6.1 %collective-permute-done.1 = f32[256,512]{1,0:T(8,128)S(1)} collective-permute-done((f32[256,512]{1,0:T(8,128)S(1)}, f32[256,512]{1,0:T(8,128)S(1)}, u32[]{:S(2)}, u32[]{:S(2)}) %collective-permute-start.1) | collective-permute-done | bytes 524320 | tf_op jit(solution)/shard_map/ppermute | solution.py:18
  64.5 1.0 %convolution_select_fusion = f32[512,256]{1,0:T(8,128)S(1)} fusion(f32[256,512]{1,0:T(8,128)S(1)} %collective-permute-done.1, f32[1,1,256,512]{3,2,1,0:T(8,128)S(1)} %copy-done.2, f32[512,256]{1,0:T(8,128)S(1)} %fusion.3, f32[1,1,256,256]{3,2,1,0:T(8,128)S(1)} %copy-done.1, f32[512]{0:T(512)S(1)} %add_sqrt_fusion, pred[]{:T(512)S(6)} %eq.23, pred[]{:T(512)S(6)} %eq.24), kind=kOutput, calls=%fused_computation.4 | convolution fusion | flops 403177472 | bytes 2361346 | tf_op jit(solution)/shard_map/dot_general | solution.py:22
  65.5 0.6 convolution_bitcast_fusion.1
  66.1 1.3 %collective-permute-start.2 = (f32[256,512]{0,1:T(8,128)S(1)}, f32[256,512]{0,1:T(8,128)S(1)}, u32[]{:S(2)}, u32[]{:S(2)}) collective-permute-start(f32[256,512]{0,1:T(8,128)S(1)} %convolution_bitcast_fusion.1), channel_id=1, source_target_pairs={{16,0},{17,1},{18,2},{19,3},{20,4},{21,5},{22,6},{23,7},{24,8},{25... | collective-permute-start | bytes 1572872 | tf_op jit(solution)/shard_map/ppermute | solution.py:18
  67.4 8.8 %collective-permute-done.2 = f32[256,512]{0,1:T(8,128)S(1)} collective-permute-done((f32[256,512]{0,1:T(8,128)S(1)}, f32[256,512]{0,1:T(8,128)S(1)}, u32[]{:S(2)}, u32[]{:S(2)}) %collective-permute-start.2) | collective-permute-done | bytes 524320 | tf_op jit(solution)/shard_map/ppermute | solution.py:18
  76.2 7.0 %collective-permute-start.3 = (f32[256,512]{0,1:T(8,128)S(1)}, f32[256,512]{0,1:T(8,128)S(1)}, u32[]{:S(2)}, u32[]{:S(2)}) collective-permute-start(f32[256,512]{0,1:T(8,128)S(1)} %collective-permute-done.2), channel_id=1, source_target_pairs={{0,15},{1,0},{2,1},{3,2},{4,3},{5,4},{6,5},{7,6},{8,7},{9,8},{10,9... | collective-permute-start | bytes 1572872 | tf_op jit(solution)/shard_map/ppermute | solution.py:12
  83.2 0.2 fusion.20
  83.4 0.6 fusion.22
  84.0 12.0 %collective-permute-done.3 = f32[256,512]{0,1:T(8,128)S(1)} collective-permute-done((f32[256,512]{0,1:T(8,128)S(1)}, f32[256,512]{0,1:T(8,128)S(1)}, u32[]{:S(2)}, u32[]{:S(2)}) %collective-permute-start.3) | collective-permute-done | bytes 524320 | tf_op jit(solution)/shard_map/ppermute | solution.py:12
  96.0 0.6 fusion.2
  96.6 0.6 fusion.1
  97.2 1.0 %copy.11 = f32[1,1,256,512]{3,2,1,0:T(8,128)} copy(f32[1,1,256,512]{2,3,1,0:T(8,128)S(1)} %fusion.1) | data formatting | bytes 1048576 | tf_op jit(solution)/shard_map/broadcast_in_dim | solution.py:77
  (10 shorter events, 0.2 us)
Async XLA Ops:
  0.0 41.8 %copy-start = (f32[1,1,4,128,256]{4,3,2,1,0:T(8,128)S(1)}, f32[1,1,4,128,256]{4,3,2,1,0:T(8,128)}, u32[]{:S(2)}) copy-start(f32[1,1,4,128,256]{4,3,2,1,0:T(8,128)} %param.5) | copy-start | bytes 1572868
  41.8 0.7 copy-start.3
  43.3 1.0 copy-start.1
  43.3 1.1 %copy-start.2 = (f32[1,1,256,512]{3,2,1,0:T(8,128)S(1)}, f32[1,1,256,512]{3,2,1,0:T(8,128)}, u32[]{:S(2)}) copy-start(f32[1,1,256,512]{3,2,1,0:T(8,128)} %param.7) | copy-start | bytes 1572868
  46.5 9.5 %collective-permute-start = (f32[256,512]{1,0:T(8,128)S(1)}, f32[256,512]{1,0:T(8,128)S(1)}, u32[]{:S(2)}, u32[]{:S(2)}) collective-permute-start(f32[256,512]{1,0:T(8,128)S(1)} %slice.25), channel_id=1, source_target_pairs={{0,1},{1,2},{2,3},{3,4},{4,5},{5,6},{6,7},{7,8},{8,9},{9,10},{10,1... | collective-permute-start | bytes 1572872 | tf_op jit(solution)/shard_map/ppermute | solution.py:12
  56.2 8.3 %collective-permute-start.1 = (f32[256,512]{1,0:T(8,128)S(1)}, f32[256,512]{1,0:T(8,128)S(1)}, u32[]{:S(2)}, u32[]{:S(2)}) collective-permute-start(f32[256,512]{1,0:T(8,128)S(1)} %slice_add_fusion), channel_id=1, source_target_pairs={{0,16},{1,17},{2,18},{3,19},{4,20},{5,21},{6,22},{7,23},{8,24},{9,... | collective-permute-start | bytes 1572872 | tf_op jit(solution)/shard_map/ppermute | solution.py:18
  66.1 10.1 %collective-permute-start.2 = (f32[256,512]{0,1:T(8,128)S(1)}, f32[256,512]{0,1:T(8,128)S(1)}, u32[]{:S(2)}, u32[]{:S(2)}) collective-permute-start(f32[256,512]{0,1:T(8,128)S(1)} %convolution_bitcast_fusion.1), channel_id=1, source_target_pairs={{16,0},{17,1},{18,2},{19,3},{20,4},{21,5},{22,6},{23,7},{24,8},{25... | collective-permute-start | bytes 1572872 | tf_op jit(solution)/shard_map/ppermute | solution.py:18
  76.2 19.9 %collective-permute-start.3 = (f32[256,512]{0,1:T(8,128)S(1)}, f32[256,512]{0,1:T(8,128)S(1)}, u32[]{:S(2)}, u32[]{:S(2)}) collective-permute-start(f32[256,512]{0,1:T(8,128)S(1)} %collective-permute-done.2), channel_id=1, source_target_pairs={{0,15},{1,0},{2,1},{3,2},{4,3},{5,4},{6,5},{7,6},{8,7},{9,8},{10,9... | collective-permute-start | bytes 1572872 | tf_op jit(solution)/shard_map/ppermute | solution.py:12
where the time goes:
time: 98.8 us; the launch traced here: 98.2 us
  blocking collectives  40.6 us (41%)
  waiting for transfers between devices  33 us (33%)
  starting transfers between devices  13.9 us (14%)
  matrix products  6.3 us (6%)
  local copies, waits for them, and re-layouts  3.04 us (3%)
  other arithmetic  1.25 us (1%)
    psum x1, blocking collectives, per_device(): norm_total = lax.psum(partial_value, ('level', 'sub'))  40.6 us
    ppermute x2, waiting for transfers between devices, passed_along(): return lax.ppermute(value, axis, pairs)  18.1 us
    ppermute x2, waiting for transfers between devices, shifted(): return lax.ppermute(block, axis, route)  14.9 us
    ppermute x2, starting transfers between devices, passed_along(): return lax.ppermute(value, axis, pairs)  10.4 us
    ppermute x2, starting transfers between devices, shifted(): return lax.ppermute(block, axis, route)  3.49 us
    dot_general x3, matrix products, apply_plain(): jnp.dot(matrix, values, precision=FULL_PRECISION, preferred_element_type=...  3.05 us
    dot_general x4, matrix products, apply_turned(): lax.dot_general(matrix, values, (((0,), (0,)), ((), ())), precision=FULL_...  2.36 us
  transfers between devices with their start and end apart: 4, of which 4 were waited for; matrix products, arithmetic and copies ran while one was open for 1% of the time, Pallas kernels for 0%

commit v1 on v0

v1 whole, which is shorter than its diff:
```python
import functools

import jax
import jax.numpy as jnp
from jax import lax
from jax.experimental import pallas as pl
from jax.experimental.pallas import tpu as pltpu
from jax.sharding import PartitionSpec as P

LANES = 128
MESH = pl.DeviceIdType.MESH


def halves(value):
    high = value.astype(jnp.bfloat16)
    low = (value - high.astype(jnp.float32)).astype(jnp.bfloat16)
    return high, low


def left_operand(matrix):
    high, low = halves(matrix)
    return jnp.concatenate([high, low, high], axis=1)


def right_operand(values):
    high, low = halves(values)
    return jnp.concatenate([high, high, low], axis=0)


def product(left, right):
    return jnp.dot(left, right, preferred_element_type=jnp.float32)


def flipped(index, bit):
    return index + bit - 2 * bit * lax.rem(lax.div(index, bit), 2)


def kernel(
    levels,
    subs,
    rows_ref,
    inverse_hbm,
    blocks_hbm,
    rhs_hbm,
    x_ref,
    total_ref,
    inverse,
    blocks,
    rhs,
    spread_own,
    spread_next,
    turned_own,
    turned_next,
    gram,
    base,
    next_out,
    next_in,
    up_out,
    up_in,
    own_in,
    beside_in,
    solved,
    sums_out,
    sums_in,
    load_sem,
    next_send,
    next_recv,
    up_send,
    up_recv,
    down_send,
    down_recv,
    side_send,
    side_recv,
    sums_send,
    sums_recv,
):
    level = lax.axis_index("level")
    sub = lax.axis_index("sub")
    chunks = rhs.shape[0]
    width = inverse.shape[0]
    slots = blocks.shape[0]
    right = lax.rem(sub + 1, subs)
    left = lax.rem(sub + subs - 1, subs)
    has_up = level < levels - 1
    has_down = level > 0
    above = {"level": level + 1}
    below = {"level": level - 1}

    loads = [
        pltpu.make_async_copy(blocks_hbm, blocks, load_sem.at[0]),
        pltpu.make_async_copy(inverse_hbm, inverse, load_sem.at[1]),
    ]
    for c in range(chunks):
        loads.append(
            pltpu.make_async_copy(
                rhs_hbm.at[:, pl.ds(c * LANES, LANES)], rhs.at[c], load_sem.at[2 + c]
            )
        )
    for load in loads:
        load.start()

    partners = []
    bit = 1
    while bit < subs:
        partners.append({"sub": flipped(sub, bit)})
        bit *= 2
    assert bit == subs
    sub_rounds = len(partners)
    bit = 1
    while bit < levels:
        partners.append({"level": flipped(level, bit)})
        bit *= 2
    assert bit == levels
    rounds = len(partners)

    barrier = pltpu.get_barrier_semaphore()
    for partner in partners:
        pl.semaphore_signal(barrier, inc=1, device_id=partner, device_id_type=MESH)

    @pl.when(has_up)
    def _():
        for partner in (above, {"sub": right}, {"sub": left}):
            pl.semaphore_signal(barrier, inc=1, device_id=partner, device_id_type=MESH)

    @pl.when(has_down)
    def _():
        pl.semaphore_signal(barrier, inc=1, device_id=below, device_id_type=MESH)

    def remote(source, target, send, recv, device):
        return pltpu.make_async_remote_copy(
            src_ref=source,
            dst_ref=target,
            send_sem=send,
            recv_sem=recv,
            device_id=device,
            device_id_type=MESH,
        )

    next_copy = [
        remote(next_out.at[c], next_in.at[c], next_send.at[c], next_recv.at[c], {"sub": right})
        for c in range(chunks)
    ]
    up_copy = [
        remote(up_out.at[c], up_in.at[c], up_send.at[c], up_recv.at[c], above)
        for c in range(chunks)
    ]
    down_copy = [
        remote(solved.at[c], own_in.at[c], down_send.at[c], down_recv.at[c], below)
        for c in range(chunks)
    ]
    side_copy = [
        remote(own_in.at[c], beside_in.at[c], side_send.at[c], side_recv.at[c], {"sub": left})
        for c in range(chunks)
    ]
    sums_copy = [
        remote(sums_out.at[r], sums_in.at[r], sums_send.at[r], sums_recv.at[r], partners[r])
        for r in range(rounds)
    ]

    loads[0].wait()
    loads[1].wait()

    def placed(slot):
        found = jnp.int32(0)
        for k in range(slots):
            found = jnp.where(rows_ref[k] == slot, k, found)
        return blocks[found]

    def spread_matrix(first):
        picked = [placed(first + d) for d in range(slots // 2)]
        ordered = jnp.concatenate(picked, axis=0)
        return product(left_operand(ordered), right_operand(inverse[...]))

    def make_next():
        matrix = spread_matrix(slots // 2)
        spread_next[...] = left_operand(matrix)
        turned_next[...] = left_operand(matrix.T)

    def make_own():
        matrix = spread_matrix(0)
        spread_own[...] = left_operand(matrix)
        turned_own[...] = left_operand(matrix.T)

    def make_gram():
        gram[...] = product(left_operand(inverse[...].T), right_operand(inverse[...]))

    def make_base(operand, c):
        base[c] = product(left_operand(gram[...]), operand)

    @pl.when(has_up)
    def _():
        make_next()

    for load in loads[2:]:
        load.wait()

    greetings = rounds + jnp.where(has_up, 3, 0) + jnp.where(has_down, 1, 0)
    pl.semaphore_wait(barrier, greetings)

    def start_sums():
        for c in range(chunks):
            value = rhs[c]
            squares = (value * value).reshape(width // 8, 8, LANES)
            sums_out[0, :, pl.ds(c * LANES, LANES)] = jnp.sum(squares, axis=0)
        sums_copy[0].start()

    def next_sums(r):
        if r >= rounds:
            return
        sums_copy[r - 1].wait_recv()
        sums_out[r] = sums_out[r - 1] + sums_in[r - 1]
        sums_copy[r].start()

    def send_next(operand, c):
        next_out[c] = product(spread_next[...], operand)
        next_copy[c].start()

    def send_up(operand, c):
        value = product(spread_own[...], operand)
        next_copy[c].wait_recv()
        up_out[c] = value + next_in[c]
        up_copy[c].start()

    @pl.when(level == 0)
    def _():
        for c in range(chunks):
            send_next(right_operand(rhs[c]), c)
        make_own()
        start_sums()
        for c in range(chunks):
            send_up(right_operand(rhs[c]), c)
            if c + 1 < sub_rounds:
                next_sums(c + 1)
        make_gram()
        for r in range(chunks + 1, sub_rounds):
            next_sums(r)
        for c in range(chunks):
            make_base(right_operand(rhs[c]), c)
        next_sums(sub_rounds)

    @pl.when(has_down)
    def _():
        start_sums()
        make_gram()

        @pl.when(has_up)
        def _():
            make_own()

        for r in range(1, sub_rounds + 1):
            next_sums(r)
        for c in range(chunks):
            up_copy[c].wait_recv()
            operand = right_operand(rhs[c] - up_in[c])

            @pl.when(has_up)
            def _():
                send_next(operand, c)
                send_up(operand, c)

            make_base(operand, c)

            @pl.when(jnp.logical_not(has_up))
            def _():
                value = base[c]
                solved[c] = value
                down_copy[c].start()
                x_ref[:, pl.ds(c * LANES, LANES)] = value

    @pl.when(has_up)
    def _():
        for c in range(chunks):
            down_copy[c].wait_recv()
            side_copy[c].start()
            value = base[c] - product(turned_own[...], right_operand(own_in[c]))
            side_copy[c].wait_recv()
            value = value - product(turned_next[...], right_operand(beside_in[c]))
            x_ref[:, pl.ds(c * LANES, LANES)] = value

            @pl.when(has_down)
            def _():
                solved[c] = value
                down_copy[c].start()

    for r in range(sub_rounds + 1, rounds):
        next_sums(r)
    sums_copy[rounds - 1].wait_recv()
    total_ref[...] = sums_out[rounds - 1] + sums_in[rounds - 1]

    for r in range(rounds):
        sums_copy[r].wait_send()

    @pl.when(has_up)
    def _():
        for c in range(chunks):
            next_copy[c].wait_send()
            up_copy[c].wait_send()
            side_copy[c].wait_send()

    @pl.when(has_down)
    def _():
        for c in range(chunks):
            down_copy[c].wait_send()


def per_device(factor_inv, update_blocks, update_rows, right_side):
    levels = lax.axis_size("level")
    subs = lax.axis_size("sub")
    width = factor_inv.shape[-1]
    columns = right_side.shape[-1]
    slots, block_rows = update_blocks.shape[2:4]
    chunks = columns // LANES
    rounds = (levels * subs).bit_length() - 1
    piece = pltpu.VMEM((chunks, width, LANES), jnp.float32)
    wide = pltpu.VMEM((width, 3 * width), jnp.bfloat16)
    chunk_sem = pltpu.SemaphoreType.DMA((chunks,))
    round_sem = pltpu.SemaphoreType.DMA((rounds,))
    any_space = pl.BlockSpec(memory_space=pl.ANY)
    in_vmem = pl.BlockSpec(memory_space=pltpu.VMEM)
    value, total = pl.pallas_call(
        functools.partial(kernel, levels, subs),
        out_shape=[
            jax.ShapeDtypeStruct((width, columns), jnp.float32),
            jax.ShapeDtypeStruct((8, columns), jnp.float32),
        ],
        in_specs=[
            pl.BlockSpec(memory_space=pltpu.SMEM),
            any_space,
            any_space,
            any_space,
        ],
        out_specs=[in_vmem, in_vmem],
        scratch_shapes=[
            pltpu.VMEM((width, width), jnp.float32),
            pltpu.VMEM((slots, block_rows, width), jnp.float32),
            piece,
            wide,
            wide,
            wide,
            wide,
            pltpu.VMEM((width, width), jnp.float32),
            piece,
            piece,
            piece,
            piece,
            piece,
            piece,
            piece,
            piece,
            pltpu.VMEM((rounds, 8, columns), jnp.float32),
            pltpu.VMEM((rounds, 8, columns), jnp.float32),
            pltpu.SemaphoreType.DMA((2 + chunks,)),
        ]
        + [chunk_sem] * 8
        + [round_sem] * 2,
        compiler_params=pltpu.CompilerParams(
            collective_id=0, has_side_effects=True, vmem_limit_bytes=40 * 1024 * 1024
        ),
        name="staircase",
    )(update_rows[0, 0], factor_inv[0, 0], update_blocks[0, 0], right_side[0, 0])
    norm_total = jnp.sum(total, axis=0)
    col_scale = jnp.sqrt(norm_total / (levels * subs * width) + 1e-06)
    return (value / col_scale)[None, None]


def solution(mesh):
    return jax.shard_map(
        per_device,
        mesh=mesh,
        in_specs=(
            P("level", "sub", None, None),
            P("level", "sub", None, None, None),
            P("level", "sub", None),
            P("level", "sub", None, None),
        ),
        out_specs=P("level", "sub", None, None),
        check_vma=False,
    )
```

time: 98.8 us -> 36.8 us (0.37)
  blocking collectives: 40.6 us -> 0 us
  waiting for transfers between devices: 33 us -> 0 us
  Pallas kernels: 0 us -> 32 us
  starting transfers between devices: 13.9 us -> 0 us
  matrix products: 6.3 us -> 0 us
    psum x1 -> x0, blocking collectives: 40.6 us -> none  [per_device(): norm_total = lax.psum(partial_value, ('level', 'sub'))]
    ppermute x4 -> x0, waiting for transfers between devices: 33 us -> none  [the longest x2 18.1 us: passed_along(): return lax.ppermute(value, axis, pairs)]
    pallas_call x0 -> x1, Pallas kernels: none -> 32 us  [per_device(): pl.pallas_call(functools.partial(kernel, levels, subs), out_shape=[jax.Sh...]
    ppermute x4 -> x0, starting transfers between devices: 13.9 us -> none  [the longest x2 10.4 us: passed_along(): return lax.ppermute(value, axis, pairs)]
    dot_general x8 -> x0, matrix products: 6.3 us -> none  [the longest x3 3.05 us: apply_plain(): jnp.dot(matrix, values, precision=FULL_PRECISION, preferred_element_type=...]
    unnamed x8, local copies, waits for them, and re-layouts: 1.66 us -> 3.69 us
    reduce_sum x1, other arithmetic: 1.16 us -> 0.02 us  [per_device(): norm_total = jnp.sum(total, axis=0)]
    broadcast_in_dim x1 -> x0, local copies, waits for them, and re-layouts: 1 us -> none  [per_device(): return result[None, None]]
  transfers between devices with their start and end apart: 4 -> 0, of which waited for: 4 -> 0; matrix products, arithmetic and copies ran while one was open for 1% -> 0% of each run, Pallas kernels for 0% -> 0%
where the time goes in v1:
time: 36.8 us; the launch traced here: 36.5 us
  Pallas kernels  32 us (87%)
  local copies, waits for them, and re-layouts  3.69 us (10%)
  other arithmetic  0.89 us (2%)
    pallas_call x1, Pallas kernels, per_device(): pl.pallas_call(functools.partial(kernel, levels, subs), out_shape=[jax.Sh...  32 us
    unnamed x8, local copies, waits for them, and re-layouts  3.69 us
    broadcast_in_dim x1, other arithmetic, per_device(): return (value / col_scale)[None, None]  0.86 us

profile of v1, /device:TPU:1, one launch (start us, length us, event | category | flops | bytes accessed | tf_op | source)
XLA Modules:
  0.0 36.5 jit_solution(14588191484346758248)
XLA Ops:
  0.0 0.0 copy-start.3
  0.0 0.7 %copy-done.3 = s32[1,1,4]{2,1,0:T(1,128)S(1)} copy-done((s32[1,1,4]{2,1,0:T(1,128)S(1)}, s32[1,1,4]{2,1,0:T(1,128)}, u32[]{:S(2)}) %copy-start.3) | copy-done | bytes 40
  0.7 0.0 copy-start
  0.7 1.0 %copy-done = f32[1,1,4,128,256]{4,3,2,1,0:T(8,128)S(1)} copy-done((f32[1,1,4,128,256]{4,3,2,1,0:T(8,128)S(1)}, f32[1,1,4,128,256]{4,3,2,1,0:T(8,128)}, u32[]{:S(2)}) %copy-start) | copy-done | bytes 524312
  1.7 0.0 copy-start.1
  1.7 1.0 %copy-done.1 = f32[1,1,256,512]{3,2,1,0:T(8,128)S(1)} copy-done((f32[1,1,256,512]{3,2,1,0:T(8,128)S(1)}, f32[1,1,256,512]{3,2,1,0:T(8,128)}, u32[]{:S(2)}) %copy-start.1) | copy-done | bytes 524312
  2.7 0.0 copy-start.2
  2.7 0.9 %copy-done.2 = f32[1,1,256,256]{3,2,1,0:T(8,128)S(1)} copy-done((f32[1,1,256,256]{3,2,1,0:T(8,128)S(1)}, f32[1,1,256,256]{3,2,1,0:T(8,128)}, u32[]{:S(2)}) %copy-start.2) | copy-done | bytes 262168
  3.7 32.0 %staircase.1 = (f32[256,512]{1,0:T(8,128)S(1)}, f32[8,512]{1,0:T(8,128)S(1)}) custom-call(s32[4]{0:T(128)S(1)} %bitcast.9, f32[256,256]{1,0:T(8,128)S(1)} %bitcast.8, f32[4,128,256]{2,1,0:T(8,128)S(1)} %bitcast.6, f32[256,512]{1,0:T(8,128)S(1)} %bitcast.7), custom_call_target="tpu_custom_call" | custom-call | tf_op jit(solution)/shard_map/staircase/pallas_call | solution.py:320
  35.7 0.9 %divide_bitcast_fusion = f32[1,1,256,512]{3,2,1,0:T(8,128)} fusion(f32[256,512]{1,0:T(8,128)S(1)} %get-tuple-element.7, f32[512]{0:T(512)S(1)} %add_sqrt_fusion), kind=kLoop, calls=%fused_computation | loop fusion | flops 131072 | bytes 1050624 | tf_op jit(solution)/shard_map/broadcast_in_dim | solution.py:363
  (2 shorter events, 0.0 us)
Async XLA Ops:
  0.0 0.7 %copy-start.3 = (s32[1,1,4]{2,1,0:T(1,128)S(1)}, s32[1,1,4]{2,1,0:T(1,128)}, u32[]{:S(2)}) copy-start(s32[1,1,4]{2,1,0:T(1,128)} %param.6) | copy-start | bytes 52
  0.7 1.0 %copy-start = (f32[1,1,4,128,256]{4,3,2,1,0:T(8,128)S(1)}, f32[1,1,4,128,256]{4,3,2,1,0:T(8,128)}, u32[]{:S(2)}) copy-start(f32[1,1,4,128,256]{4,3,2,1,0:T(8,128)} %param.5) | copy-start | bytes 1572868
  1.7 1.0 %copy-start.1 = (f32[1,1,256,512]{3,2,1,0:T(8,128)S(1)}, f32[1,1,256,512]{3,2,1,0:T(8,128)}, u32[]{:S(2)}) copy-start(f32[1,1,256,512]{3,2,1,0:T(8,128)} %param.7) | copy-start | bytes 1572868
  2.7 0.9 %copy-start.2 = (f32[1,1,256,256]{3,2,1,0:T(8,128)S(1)}, f32[1,1,256,256]{3,2,1,0:T(8,128)}, u32[]{:S(2)}) copy-start(f32[1,1,256,256]{3,2,1,0:T(8,128)} %param.4) | copy-start | bytes 786436

commit v2 on v1

v2 whole, which is shorter than its diff:
```python
import functools

import jax
import jax.numpy as jnp
from jax import lax
from jax.experimental import pallas as pl
from jax.experimental.pallas import tpu as pltpu
from jax.sharding import PartitionSpec as P

LANES = 128
MESH = pl.DeviceIdType.MESH


def halves(value):
    high = value.astype(jnp.bfloat16)
    low = (value - high.astype(jnp.float32)).astype(jnp.bfloat16)
    return high, low


def left_operand(matrix):
    high, low = halves(matrix)
    return jnp.concatenate([high, low, high], axis=1)


def right_operand(values):
    high, low = halves(values)
    return jnp.concatenate([high, high, low], axis=0)


def product(left, right):
    return jnp.dot(left, right, preferred_element_type=jnp.float32)


def flipped(index, bit):
    return index + bit - 2 * bit * lax.rem(lax.div(index, bit), 2)


def kernel(
    levels,
    subs,
    rows_ref,
    inverse_hbm,
    blocks_hbm,
    rhs_hbm,
    x_ref,
    total_ref,
    inverse,
    blocks,
    rhs,
    spread_own,
    spread_next,
    turned_own,
    turned_next,
    gram,
    gram_top,
    base,
    own,
    next_out,
    next_in,
    up_in,
    own_in,
    beside_in,
    solved,
    top_corner,
    top_rows,
    top_rhs,
    sums_out,
    sums_in,
    load_sem,
    give_send,
    give_recv,
    next_send,
    next_recv,
    up_send,
    up_recv,
    down_send,
    down_recv,
    side_send,
    side_recv,
    sums_send,
    sums_recv,
):
    level = lax.axis_index("level")
    sub = lax.axis_index("sub")
    chunks = rhs.shape[0]
    width = inverse.shape[0]
    half = width // 2
    slots = blocks.shape[0]
    right = lax.rem(sub + 1, subs)
    left = lax.rem(sub + subs - 1, subs)
    is_top = level == levels - 1
    is_host = level == levels - 2
    has_up = level < levels - 1
    above = {"level": level + 1}
    below = {"level": level - 1}

    block_load = pltpu.make_async_copy(blocks_hbm, blocks, load_sem.at[0])
    inverse_load = pltpu.make_async_copy(inverse_hbm, inverse, load_sem.at[1])
    rhs_loads = [
        pltpu.make_async_copy(
            rhs_hbm.at[:, pl.ds(c * LANES, LANES)], rhs.at[c], load_sem.at[2 + c]
        )
        for c in range(chunks)
    ]

    @pl.when(has_up)
    def _():
        block_load.start()
        inverse_load.start()

    for load in rhs_loads:
        load.start()

    partners = []
    bit = 1
    while bit < subs:
        partners.append({"sub": flipped(sub, bit)})
        bit *= 2
    assert bit == subs
    sub_rounds = len(partners)
    bit = 1
    while bit < levels:
        partners.append({"level": flipped(level, bit)})
        bit *= 2
    assert bit == levels
    rounds = len(partners)

    barrier = pltpu.get_barrier_semaphore()
    for partner in partners:
        pl.semaphore_signal(barrier, inc=1, device_id=partner, device_id_type=MESH)

    @pl.when(has_up)
    def _():
        for partner in (above, {"sub": right}, {"sub": left}):
            pl.semaphore_signal(barrier, inc=1, device_id=partner, device_id_type=MESH)

    @pl.when(level > 0)
    def _():
        pl.semaphore_signal(barrier, inc=1, device_id=below, device_id_type=MESH)

    def remote(source, target, send, recv, device):
        return pltpu.make_async_remote_copy(
            src_ref=source,
            dst_ref=target,
            send_sem=send,
            recv_sem=recv,
            device_id=device,
            device_id_type=MESH,
        )

    def chunk_copies(source, target, send, recv, device):
        return [
            remote(source.at[c], target.at[c], send.at[c], recv.at[c], device)
            for c in range(chunks)
        ]

    give_copy = [
        remote(
            inverse_hbm.at[pl.ds(0, half), pl.ds(0, half)],
            top_corner,
            give_send.at[0],
            give_recv.at[0],
            below,
        ),
        remote(
            inverse_hbm.at[pl.ds(half, half)], top_rows, give_send.at[1], give_recv.at[1], below
        ),
    ]
    for c in range(chunks):
        give_copy.append(
            remote(
                rhs_hbm.at[:, pl.ds(c * LANES, LANES)],
                top_rhs.at[c],
                give_send.at[2 + c],
                give_recv.at[2 + c],
                below,
            )
        )
    next_copy = chunk_copies(next_out, next_in, next_send, next_recv, {"sub": right})
    up_copy = chunk_copies(own, up_in, up_send, up_recv, above)
    lift_copy = chunk_copies(own_in, solved, up_send, up_recv, above)
    down_copy = chunk_copies(solved, own_in, down_send, down_recv, below)
    side_copy = chunk_copies(own_in, beside_in, side_send, side_recv, {"sub": left})
    sums_copy = [
        remote(sums_out.at[r], sums_in.at[r], sums_send.at[r], sums_recv.at[r], partners[r])
        for r in range(rounds)
    ]

    def placed(slot):
        found = jnp.int32(0)
        for k in range(slots):
            found = jnp.where(rows_ref[k] == slot, k, found)
        return blocks[found]

    def spread_matrix(first):
        picked = [placed(first + d) for d in range(slots // 2)]
        ordered = jnp.concatenate(picked, axis=0)
        return product(left_operand(ordered), right_operand(inverse[...]))

    def squared(matrix):
        return left_operand(product(left_operand(matrix.T), right_operand(matrix)))

    def start_sums():
        for c in range(chunks):
            value = rhs[c]
            squares = (value * value).reshape(width // 8, 8, LANES)
            sums_out[0, :, pl.ds(c * LANES, LANES)] = jnp.sum(squares, axis=0)
        sums_copy[0].start()

    def next_sums(r):
        if r < rounds:
            sums_copy[r - 1].wait_recv()
            sums_out[r] = sums_out[r - 1] + sums_in[r - 1]
            sums_copy[r].start()

    def store(c, value):
        x_ref[:, pl.ds(c * LANES, LANES)] = value

    greetings = rounds + jnp.where(has_up, 3, 0) + jnp.where(level > 0, 1, 0)

    @pl.when(is_top)
    def _():
        pl.semaphore_wait(barrier, greetings)
        for copy in give_copy:
            copy.start()
        for load in rhs_loads:
            load.wait()
        start_sums()
        for r in range(1, sub_rounds + 1):
            next_sums(r)
        for c in range(chunks):
            lift_copy[c].wait_recv()
            store(c, solved[c])
        for copy in give_copy:
            copy.wait_send()

    def make_next():
        matrix = spread_matrix(slots // 2)
        spread_next[...] = left_operand(matrix)

    def make_own():
        matrix = spread_matrix(0)
        spread_own[...] = left_operand(matrix)

    def make_turned():
        for matrix, turned in ((spread_own, turned_own), (spread_next, turned_next)):
            for piece in range(3):
                span = pl.ds(piece * width, width)
                turned[:, span] = matrix[:, span].T

    def send_next(operand, c):
        next_out[c] = product(spread_next[...], operand)
        next_copy[c].start()

    def finish(c):
        side_copy[c].wait_recv()
        value = base[c] - product(turned_next[...], right_operand(beside_in[c]))
        store(c, value)
        if levels > 2:

            @pl.when(level > 0)
            def _():
                solved[c] = value
                down_copy[c].start()

    @pl.when(has_up)
    def _():
        block_load.wait()
        inverse_load.wait()
        make_next()
        for load in rhs_loads:
            load.wait()
        pl.semaphore_wait(barrier, greetings)

    @pl.when(is_host)
    def _():
        if levels > 2:

            @pl.when(level > 0)
            def _():
                for c in range(chunks):
                    up_copy[c].wait_recv()

        def remaining(c):
            if levels == 2:
                return rhs[c]
            return rhs[c] - jnp.where(level > 0, up_in[c], 0.0)

        for c in range(chunks):
            send_next(right_operand(remaining(c)), c)
        start_sums()
        make_own()
        next_sums(1)
        gram[...] = squared(inverse[...])
        for c in range(chunks):
            operand = right_operand(remaining(c))
            own[c] = product(spread_own[...], operand)
            base[c] = product(gram[...], operand)
            if c + 2 < sub_rounds:
                next_sums(c + 2)
        for r in range(chunks + 2, sub_rounds):
            next_sums(r)
        make_turned()
        give_copy[0].wait_recv()
        give_copy[1].wait_recv()
        corner = jnp.concatenate([top_corner[...], jnp.zeros((half, half), jnp.float32)], axis=1)
        gram_top[...] = squared(jnp.concatenate([corner, top_rows[...]], axis=0))
        for c in range(chunks):
            next_copy[c].wait_recv()
            give_copy[2 + c].wait_recv()
            operand = right_operand(top_rhs[c] - (own[c] + next_in[c]))
            value = product(gram_top[...], operand)
            own_in[c] = value
            side_copy[c].start()
            lift_copy[c].start()
            base[c] = base[c] - product(turned_own[...], right_operand(value))
            if c == 0:
                next_sums(sub_rounds)
            if c > 0:
                finish(c - 1)
        finish(chunks - 1)
        for c in range(chunks):
            next_copy[c].wait_send()
            lift_copy[c].wait_send()
            side_copy[c].wait_send()

    if levels > 2:

        @pl.when(level < levels - 2)
        def _():
            make_own()
            make_turned()
            gram[...] = squared(inverse[...])
            start_sums()
            for r in range(1, sub_rounds + 1):
                next_sums(r)

            @pl.when(level > 0)
            def _():
                for c in range(chunks):
                    up_copy[c].wait_recv()

            for c in range(chunks):
                operand = right_operand(rhs[c] - jnp.where(level > 0, up_in[c], 0.0))
                send_next(operand, c)
                value = product(spread_own[...], operand)
                next_copy[c].wait_recv()
                own[c] = value + next_in[c]
                up_copy[c].start()
                base[c] = product(gram[...], operand)
            for c in range(chunks):
                down_copy[c].wait_recv()
                side_copy[c].start()
                base[c] = base[c] - product(turned_own[...], right_operand(own_in[c]))
                finish(c)
            for c in range(chunks):
                next_copy[c].wait_send()
                up_copy[c].wait_send()
                side_copy[c].wait_send()

        @pl.when(jnp.logical_and(level > 0, has_up))
        def _():
            for c in range(chunks):
                down_copy[c].wait_send()

    for r in range(sub_rounds + 1, rounds):
        next_sums(r)
    sums_copy[rounds - 1].wait_recv()
    total_ref[...] = sums_out[rounds - 1] + sums_in[rounds - 1]
    for r in range(rounds):
        sums_copy[r].wait_send()


def per_device(factor_inv, update_blocks, update_rows, right_side):
    levels = lax.axis_size("level")
    subs = lax.axis_size("sub")
    width = factor_inv.shape[-1]
    columns = right_side.shape[-1]
    slots, block_rows = update_blocks.shape[2:4]
    chunks = columns // LANES
    rounds = (levels * subs).bit_length() - 1
    piece = pltpu.VMEM((chunks, width, LANES), jnp.float32)
    wide = pltpu.VMEM((width, 3 * width), jnp.bfloat16)
    chunk_sem = pltpu.SemaphoreType.DMA((chunks,))
    round_sem = pltpu.SemaphoreType.DMA((rounds,))
    any_space = pl.BlockSpec(memory_space=pltpu.HBM)
    in_vmem = pl.BlockSpec(memory_space=pltpu.VMEM)
    value, total = pl.pallas_call(
        functools.partial(kernel, levels, subs),
        out_shape=[
            jax.ShapeDtypeStruct((width, columns), jnp.float32),
            jax.ShapeDtypeStruct((8, columns), jnp.float32),
        ],
        in_specs=[
            pl.BlockSpec(memory_space=pltpu.SMEM),
            any_space,
            any_space,
            any_space,
        ],
        out_specs=[in_vmem, in_vmem],
        scratch_shapes=[
            pltpu.VMEM((width, width), jnp.float32),
            pltpu.VMEM((slots, block_rows, width), jnp.float32),
            piece,
        ]
        + [wide] * 6
        + [piece] * 8
        + [
            pltpu.VMEM((width // 2, width // 2), jnp.float32),
            pltpu.VMEM((width // 2, width), jnp.float32),
            piece,
            pltpu.VMEM((rounds, 8, columns), jnp.float32),
            pltpu.VMEM((rounds, 8, columns), jnp.float32),
        ]
        + [pltpu.SemaphoreType.DMA((2 + chunks,))] * 3
        + [chunk_sem] * 8
        + [round_sem] * 2,
        compiler_params=pltpu.CompilerParams(
            collective_id=0, has_side_effects=True, vmem_limit_bytes=60 * 1024 * 1024
        ),
        name="staircase",
    )(update_rows[0, 0], factor_inv[0, 0], update_blocks[0, 0], right_side[0, 0])
    norm_total = jnp.sum(total, axis=0)
    col_scale = jnp.sqrt(norm_total / (levels * subs * width) + 1e-06)
    return (value / col_scale)[None, None]


def solution(mesh):
    return jax.shard_map(
        per_device,
        mesh=mesh,
        in_specs=(
            P("level", "sub", None, None),
            P("level", "sub", None, None, None),
            P("level", "sub", None),
            P("level", "sub", None, None),
        ),
        out_specs=P("level", "sub", None, None),
        check_vma=False,
    )
```

time: 36.8 us -> 33.9 us (0.921)
  the two profiles are of different devices: /device:TPU:1 before, /device:TPU:12 now
where the time goes in v2:
time: 33.9 us; the launch traced here: 33.7 us
  Pallas kernels  31 us (91%)
  other arithmetic  2.65 us (8%)
    pallas_call x1, Pallas kernels, per_device(): pl.pallas_call(functools.partial(kernel, levels, subs), out_shape=[jax.Sh...  31 us
    broadcast_in_dim x1, other arithmetic, per_device(): return (value / col_scale)[None, None]  1.91 us
    reduce_sum x1, other arithmetic, per_device(): norm_total = jnp.sum(total, axis=0)  0.73 us

profile of v2, /device:TPU:12, one launch (start us, length us, event | category | flops | bytes accessed | tf_op | source)
XLA Modules:
  0.0 33.7 jit_solution(14801019811845400084)
XLA Ops:
  0.0 31.0 %staircase.1 = (f32[256,512]{1,0:T(8,128)}, f32[8,512]{1,0:T(8,128)}) custom-call(s32[4]{0:T(128)} %bitcast.9, f32[256,256]{1,0:T(8,128)} %bitcast.8, f32[4,128,256]{2,1,0:T(8,128)} %bitcast.6, f32[256,512]{1,0:T(8,128)} %bitcast.7), custom_call_target="tpu_custom_call" | custom-call | tf_op jit(solution)/shard_map/staircase/pallas_call | solution.py:388
  31.0 0.7 %reduce_sum.9 = f32[512]{0:T(512)S(1)} reduce(f32[8,512]{1,0:T(8,128)} %get-tuple-element.8, f32[]{:T(128)} %constant.1.clone.1), dimensions={0}, to_apply=%region_0.0 | reduce | flops 3584 | bytes 18436 | tf_op jit(solution)/shard_map/reduce_sum | solution.py:423
  31.8 1.9 %divide_bitcast_fusion = f32[1,1,256,512]{3,2,1,0:T(8,128)} fusion(f32[256,512]{1,0:T(8,128)} %get-tuple-element.7, f32[512]{0:T(512)S(1)} %add_sqrt_fusion), kind=kLoop, calls=%fused_computation | loop fusion | flops 131072 | bytes 1050624 | tf_op jit(solution)/shard_map/broadcast_in_dim | solution.py:425
  (1 shorter events, 0.0 us)

commit v3 on v2

--- a/solution.py
+++ b/solution.py
@@ -43,7 +43,7 @@
     blocks_hbm,
     rhs_hbm,
     x_ref,
-    total_ref,
+    scale_ref,
     inverse,
     blocks,
     rhs,
@@ -89,7 +89,8 @@
     right = lax.rem(sub + 1, subs)
     left = lax.rem(sub + subs - 1, subs)
     is_top = level == levels - 1
-    is_host = level == levels - 2
+    lent = lax.rem(sub, 2) == 0
+    is_host = jnp.logical_and(level == levels - 2, lent)
     has_up = level < levels - 1
     above = {"level": level + 1}
     below = {"level": level - 1}
@@ -106,8 +107,8 @@
     @pl.when(has_up)
     def _():
         block_load.start()
-        inverse_load.start()
-
+
+    inverse_load.start()
     for load in rhs_loads:
         load.start()
 
@@ -218,20 +219,48 @@
 
     greetings = rounds + jnp.where(has_up, 3, 0) + jnp.where(level > 0, 1, 0)
 
-    @pl.when(is_top)
-    def _():
+    @pl.when(jnp.logical_and(is_top, jnp.logical_not(lent)))
+    def _():
+        inverse_load.wait()
+        gram[...] = squared(inverse[...])
+        for load in rhs_loads:
+            load.wait()
         pl.semaphore_wait(barrier, greetings)
-        for copy in give_copy:
+        start_sums()
+        for c in range(chunks):
+            up_copy[c].wait_recv()
+            value = product(gram[...], right_operand(rhs[c] - up_in[c]))
+            solved[c] = value
+            down_copy[c].start()
+            store(c, value)
+            if c + 1 < sub_rounds:
+                next_sums(c + 1)
+        for r in range(chunks + 1, sub_rounds):
+            next_sums(r)
+        next_sums(sub_rounds)
+        for c in range(chunks):
+            down_copy[c].wait_send()
+
+    @pl.when(jnp.logical_and(is_top, lent))
+    def _():
+        inverse_load.wait()
+        pl.semaphore_wait(barrier, greetings)
+        for copy in give_copy[:3]:
             copy.start()
         for load in rhs_loads:
             load.wait()
         start_sums()
+        for n in range(3, 2 + chunks):
+            if n == 3:
+                give_copy[0].wait_send()
+            give_copy[n - 2].wait_send()
+            give_copy[n].start()
         for r in range(1, sub_rounds + 1):
             next_sums(r)
         for c in range(chunks):
             lift_copy[c].wait_recv()
             store(c, solved[c])
-        for copy in give_copy:
+        for copy in give_copy[chunks:]:
             copy.wait_send()
 
     def make_next():
@@ -287,20 +316,21 @@
             return rhs[c] - jnp.where(level > 0, up_in[c], 0.0)
 
         for c in range(chunks):
-            send_next(right_operand(remaining(c)), c)
+            next_out[c] = product(spread_next[...], right_operand(remaining(c)))
+            if c < 2:
+                next_copy[c].start()
         start_sums()
         make_own()
-        next_sums(1)
-        gram[...] = squared(inverse[...])
-        for c in range(chunks):
-            operand = right_operand(remaining(c))
-            own[c] = product(spread_own[...], operand)
-            base[c] = product(gram[...], operand)
-            if c + 2 < sub_rounds:
-                next_sums(c + 2)
-        for r in range(chunks + 2, sub_rounds):
-            next_sums(r)
-        make_turned()
+        for c in range(chunks):
+            own[c] = product(spread_own[...], right_operand(remaining(c)))
+        for c in range(2, chunks):
+            next_copy[c - 2].wait_send()
+            next_copy[c].start()
+            if c == 2:
+                gram[...] = squared(inverse[...])
+                make_turned()
+        for c in range(chunks):
+            base[c] = product(gram[...], right_operand(remaining(c)))
         give_copy[0].wait_recv()
         give_copy[1].wait_recv()
         corner = jnp.concatenate([top_corner[...], jnp.zeros((half, half), jnp.float32)], axis=1)
@@ -314,49 +344,66 @@
             side_copy[c].start()
             lift_copy[c].start()
             base[c] = base[c] - product(turned_own[...], right_operand(value))
-            if c == 0:
-                next_sums(sub_rounds)
+            if c + 1 < sub_rounds:
+                next_sums(c + 1)
             if c > 0:
                 finish(c - 1)
+        for r in range(chunks + 1, sub_rounds):
+            next_sums(r)
+        next_sums(sub_rounds)
         finish(chunks - 1)
         for c in range(chunks):
-            next_copy[c].wait_send()
+            if c >= chunks - 2:
+                next_copy[c].wait_send()
             lift_copy[c].wait_send()
             side_copy[c].wait_send()
 
-    if levels > 2:
-
-        @pl.when(level < levels - 2)
-        def _():
-            make_own()
-            make_turned()
-            gram[...] = squared(inverse[...])
-            start_sums()
-            for r in range(1, sub_rounds + 1):
-                next_sums(r)
+    @pl.when(jnp.logical_and(has_up, jnp.logical_not(is_host)))
+    def _():
+        if levels > 2:
 
             @pl.when(level > 0)
             def _():
                 for c in range(chunks):
                     up_copy[c].wait_recv()
 
-            for c in range(chunks):
-                operand = right_operand(rhs[c] - jnp.where(level > 0, up_in[c], 0.0))
-                send_next(operand, c)
-                value = product(spread_own[...], operand)
-                next_copy[c].wait_recv()
-                own[c] = value + next_in[c]
-                up_copy[c].start()
-                base[c] = product(gram[...], operand)
-            for c in range(chunks):
-                down_copy[c].wait_recv()
-                side_copy[c].start()
-                base[c] = base[c] - product(turned_own[...], right_operand(own_in[c]))
-                finish(c)
-            for c in range(chunks):
-                next_copy[c].wait_send()
-                up_copy[c].wait_send()
-                side_copy[c].wait_send()
+        def remaining(c):
+            if levels == 2:
+                return rhs[c]
+            return rhs[c] - jnp.where(level > 0, up_in[c], 0.0)
+
+        make_own()
+        for c in range(chunks):
+            operand = right_operand(remaining(c))
+            send_next(operand, c)
+            own[c] = product(spread_own[...], operand)
+        start_sums()
+        for c in range(chunks):
+            next_copy[c].wait_recv()
+            own[c] = own[c] + next_in[c]
+            up_copy[c].start()
+        make_turned()
+        gram[...] = squared(inverse[...])
+        for c in range(chunks):
+            base[c] = product(gram[...], right_operand(remaining(c)))
+        for c in range(chunks):
+            down_copy[c].wait_recv()
+            side_copy[c].start()
+            base[c] = base[c] - product(turned_own[...], right_operand(own_in[c]))
+            if c + 1 < sub_rounds:
+                next_sums(c + 1)
+            if c > 0:
+                finish(c - 1)
+        for r in range(chunks + 1, sub_rounds):
+            next_sums(r)
+        next_sums(sub_rounds)
+        finish(chunks - 1)
+        for c in range(chunks):
+            next_copy[c].wait_send()
+            up_copy[c].wait_send()
+            side_copy[c].wait_send()
+
+    if levels > 2:
 
         @pl.when(jnp.logical_and(level > 0, has_up))
         def _():
@@ -366,7 +413,8 @@
     for r in range(sub_rounds + 1, rounds):
         next_sums(r)
     sums_copy[rounds - 1].wait_recv()
-    total_ref[...] = sums_out[rounds - 1] + sums_in[rounds - 1]
+    total = jnp.sum(sums_out[rounds - 1] + sums_in[rounds - 1], axis=0, keepdims=True)
+    scale_ref[...] = jnp.sqrt(total / (levels * subs * width) + 1e-06)
     for r in range(rounds):
         sums_copy[r].wait_send()
 
@@ -385,11 +433,11 @@
     round_sem = pltpu.SemaphoreType.DMA((rounds,))
     any_space = pl.BlockSpec(memory_space=pltpu.HBM)
     in_vmem = pl.BlockSpec(memory_space=pltpu.VMEM)
-    value, total = pl.pallas_call(
+    value, col_scale = pl.pallas_call(
         functools.partial(kernel, levels, subs),
         out_shape=[
             jax.ShapeDtypeStruct((width, columns), jnp.float32),
-            jax.ShapeDtypeStruct((8, columns), jnp.float32),
+            jax.ShapeDtypeStruct((1, columns), jnp.float32),
         ],
         in_specs=[
             pl.BlockSpec(memory_space=pltpu.SMEM),
@@ -420,8 +468,6 @@
         ),
         name="staircase",
     )(update_rows[0, 0], factor_inv[0, 0], update_blocks[0, 0], right_side[0, 0])
-    norm_total = jnp.sum(total, axis=0)
-    col_scale = jnp.sqrt(norm_total / (levels * subs * width) + 1e-06)
     return (value / col_scale)[None, None]
 
 

time: 33.9 us -> 28.3 us (0.83)
  the two profiles are of different devices: /device:TPU:12 before, /device:TPU:1 now
where the time goes in v3:
time: 28.3 us; the launch traced here: 28.1 us
  Pallas kernels  25.5 us (90%)
  other arithmetic  1.9 us (7%)
  local copies, waits for them, and re-layouts  0.66 us (2%)
    pallas_call x1, Pallas kernels, per_device(): pl.pallas_call(functools.partial(kernel, levels, subs), out_shape=[jax.Sh...  25.5 us
    broadcast_in_dim x1, other arithmetic, per_device(): return (value / col_scale)[None, None]  1.9 us
    unnamed x2, local copies, waits for them, and re-layouts  0.66 us

profile of v3, /device:TPU:1, one launch (start us, length us, event | category | flops | bytes accessed | tf_op | source)
XLA Modules:
  0.0 28.1 jit_solution(3960422923191829643)
XLA Ops:
  0.0 25.5 %staircase.1 = (f32[256,512]{1,0:T(8,128)}, f32[1,512]{1,0:T(1,128)}) custom-call(s32[4]{0:T(128)} %bitcast.11, f32[256,256]{1,0:T(8,128)} %bitcast.9, f32[4,128,256]{2,1,0:T(8,128)} %bitcast.7, f32[256,512]{1,0:T(8,128)} %bitcast.8), custom_call_target="tpu_custom_call" | custom-call | tf_op jit(solution)/shard_map/staircase/pallas_call | solution.py:436
  25.5 0.0 copy-start
  25.5 0.7 %copy-done = f32[1,512]{1,0:T(1,128)S(1)} copy-done((f32[1,512]{1,0:T(1,128)S(1)}, f32[1,512]{1,0:T(1,128)}, u32[]{:S(2)}) %copy-start) | copy-done | bytes 2072
  26.2 1.9 %divide_bitcast_fusion = f32[1,1,256,512]{3,2,1,0:T(8,128)} fusion(f32[256,512]{1,0:T(8,128)} %get-tuple-element.7, f32[512]{0:T(512)S(1)} %bitcast.10), kind=kLoop, calls=%fused_computation | loop fusion | flops 131072 | bytes 1050624 | tf_op jit(solution)/shard_map/broadcast_in_dim | solution.py:471
Async XLA Ops:
  25.5 0.7 %copy-start = (f32[1,512]{1,0:T(1,128)S(1)}, f32[1,512]{1,0:T(1,128)}, u32[]{:S(2)}) copy-start(f32[1,512]{1,0:T(1,128)} %get-tuple-element.8) | copy-start | bytes 6148

commit v4 on v3

--- a/solution.py
+++ b/solution.py
@@ -43,7 +43,6 @@
     blocks_hbm,
     rhs_hbm,
     x_ref,
-    scale_ref,
     inverse,
     blocks,
     rhs,
@@ -414,7 +413,7 @@
         next_sums(r)
     sums_copy[rounds - 1].wait_recv()
     total = jnp.sum(sums_out[rounds - 1] + sums_in[rounds - 1], axis=0, keepdims=True)
-    scale_ref[...] = jnp.sqrt(total / (levels * subs * width) + 1e-06)
+    x_ref[...] = x_ref[...] / jnp.sqrt(total / (levels * subs * width) + 1e-06)
     for r in range(rounds):
         sums_copy[r].wait_send()
 
@@ -433,19 +432,16 @@
     round_sem = pltpu.SemaphoreType.DMA((rounds,))
     any_space = pl.BlockSpec(memory_space=pltpu.HBM)
     in_vmem = pl.BlockSpec(memory_space=pltpu.VMEM)
-    value, col_scale = pl.pallas_call(
+    value = pl.pallas_call(
         functools.partial(kernel, levels, subs),
-        out_shape=[
-            jax.ShapeDtypeStruct((width, columns), jnp.float32),
-            jax.ShapeDtypeStruct((1, columns), jnp.float32),
-        ],
+        out_shape=jax.ShapeDtypeStruct((width, columns), jnp.float32),
         in_specs=[
             pl.BlockSpec(memory_space=pltpu.SMEM),
             any_space,
             any_space,
             any_space,
         ],
-        out_specs=[in_vmem, in_vmem],
+        out_specs=in_vmem,
         scratch_shapes=[
             pltpu.VMEM((width, width), jnp.float32),
             pltpu.VMEM((slots, block_rows, width), jnp.float32),
@@ -468,7 +464,7 @@
         ),
         name="staircase",
     )(update_rows[0, 0], factor_inv[0, 0], update_blocks[0, 0], right_side[0, 0])
-    return (value / col_scale)[None, None]
+    return value[None, None]
 
 
 def solution(mesh):

time: 28.3 us -> 27.6 us (0.975)
  other arithmetic: 1.9 us -> 0 us
  local copies, waits for them, and re-layouts: 0.66 us -> 1.87 us
    broadcast_in_dim x1 -> x0, other arithmetic: 1.9 us -> none  [per_device(): return (value / col_scale)[None, None]]
    unnamed x2 -> x1, local copies, waits for them, and re-layouts: 0.66 us -> 1.87 us
where the time goes in v4:
time: 27.6 us; the launch traced here: 27.4 us
  Pallas kernels  25.6 us (93%)
  local copies, waits for them, and re-layouts  1.87 us (7%)
    pallas_call x1, Pallas kernels, per_device(): pl.pallas_call(functools.partial(kernel, levels, subs), out_shape=jax.Sha...  25.6 us
    unnamed x1, local copies, waits for them, and re-layouts  1.87 us

profile of v4, /device:TPU:1, one launch (start us, length us, event | category | flops | bytes accessed | tf_op | source)
XLA Modules:
  0.0 27.4 jit_solution(2223568444210439351)
XLA Ops:
  0.0 25.6 %staircase.1 = f32[256,512]{1,0:T(8,128)} custom-call(s32[4]{0:T(128)} %bitcast.9, f32[256,256]{1,0:T(8,128)} %bitcast.8, f32[4,128,256]{2,1,0:T(8,128)} %bitcast.6, f32[256,512]{1,0:T(8,128)} %bitcast.7), custom_call_target="tpu_custom_call" | custom-call | tf_op jit(solution)/shard_map/staircase/pallas_call | solution.py:435
  25.6 1.9 %copy.6 = f32[1,1,256,512]{3,2,1,0:T(8,128)} copy(f32[1,1,256,512]{3,2,1,0:T(8,128)} %bitcast.5) | data formatting | bytes 1048576
